TPU v7x, 32 devices: a whole 2x2x4 slice. The times are simulated.
32 devices in a mesh: sub: 16 (over z, x, core), grid: 2 (over y).
Axes of the slice: x: 2, y: 2, z: 4, core: 2. Of those that a mesh axis runs over, the one named last changes fastest.
Arguments:
- front_entries: float32 [16, 12, 128, 2, 1536], P('sub', None, None, 'grid'), as said below
- coupling_rows: bfloat16 [16, 2048, 256], P('sub', 'grid'), may hold values from -0.09375 to 0.09375
- child_map: int32 [16, 2048], P('sub'), may hold values from 0 to 3071, as said below
Outputs:
- factored: float32 [16, 12, 128, 2, 1536], P('sub', None, None, 'grid')
Inputs may be any that keep to these rules, and one draw needn't show every extreme that they name: `child_map`: rows 2 p and 2 p + 1 each hold 2048 distinct indices, and together they name every index of the parent front. `front_entries`: each front is symmetric, and stays positive definite after both children's updates are subtracted.
All inputs are finite; a program needn't handle non-finite values.
Results may differ from a plain program's by a relative error of at most 0.0003.
Values may be sent and summed in bfloat16 or wider, within the bound.
A program may use at most 128 MiB of HBM per device.

v0:
```python
import jax
import jax.numpy as jnp
from jax import lax
from jax.sharding import PartitionSpec as P

NB = 128
PF = 3072
PIV = 1024


def partner(shard, axis, apart):
    return lax.ppermute(shard, axis, [(i, i ^ 1 << apart) for i in range(lax.axis_size(axis))])


def broadcast(shard, axis, root):
    mine = lax.axis_index(axis) == root
    return lax.psum(jnp.where(mine, shard, jnp.zeros_like(shard)), axis)


def invert_map(mapping):
    return (
        jnp.full((PF,), -1, jnp.int32)
        .at[mapping]
        .set(jnp.arange(mapping.shape[0], dtype=jnp.int32))
    )


def select_rows(table, inverse, wanted):
    index = inverse[wanted]
    found = index >= 0
    picked = table[jnp.where(found, index, 0)]
    return jnp.where(found[:, None], picked, jnp.zeros((), table.dtype))


def outer_product(left, right, precision):
    return lax.dot_general(
        left,
        right,
        (((1,), (1,)), ((), ())),
        precision=precision,
        preferred_element_type=jnp.float32,
    )


def block_indices(block_ids):
    offsets = jnp.arange(NB, dtype=jnp.int32)
    return (block_ids[:, None] * NB + offsets[None, :]).reshape(-1)


def on_device(front_entries, coupling_rows, child_map):
    sibling = lax.axis_index("sub") % 2
    column_owner = lax.axis_index("grid")
    grid_count = lax.axis_size("grid")
    row_blocks = front_entries.shape[1]
    col_width = front_entries.shape[4]
    col_blocks = col_width // NB
    local = front_entries.reshape(row_blocks * NB, col_width)
    row_block_ids = jnp.arange(row_blocks, dtype=jnp.int32) * 2 + sibling
    col_block_ids = jnp.arange(col_blocks, dtype=jnp.int32) * grid_count + column_owner
    my_rows = block_indices(row_block_ids)
    my_cols = block_indices(col_block_ids)
    own_map = child_map[0]
    own_inverse = invert_map(own_map)
    everything = lax.all_gather(coupling_rows, "grid", axis=1, tiled=True)[0]
    update = outer_product(coupling_rows[0], everything, None)
    dest_blocks = (
        jnp.arange(grid_count, dtype=jnp.int32)[:, None]
        + jnp.arange(col_blocks, dtype=jnp.int32)[None, :] * grid_count
    )
    dest_cols = block_indices(dest_blocks.reshape(-1))
    col_index = own_inverse[dest_cols]
    found = col_index >= 0
    spread = jnp.where(found[None, :], update[:, jnp.where(found, col_index, 0)], 0.0)
    spread = spread.reshape(update.shape[0], grid_count, col_width)
    arrived = (
        lax.all_to_all(spread.astype(jnp.bfloat16), "grid", split_axis=1, concat_axis=0, tiled=True)
        .astype(spread.dtype)
        .reshape(-1, col_width)
    )
    partner_rows = block_indices(jnp.arange(row_blocks, dtype=jnp.int32) * 2 + (1 - sibling))
    keep = select_rows(arrived, own_inverse, my_rows)
    give = select_rows(arrived, own_inverse, partner_rows)
    received = partner(give.astype(jnp.bfloat16), "sub", 0).astype(give.dtype)
    local = local - keep - received
    highest = lax.Precision.HIGHEST
    identity = jnp.eye(NB, dtype=jnp.float32)
    col_repeat = jnp.repeat(col_block_ids, NB)
    row_repeat = jnp.repeat(row_block_ids, NB)
    for step in range(PIV // NB):
        owner = step % grid_count
        local_col = step // grid_count * NB
        first = step // 2 * NB
        column = broadcast(local[:, local_col : local_col + NB], "grid", owner)
        own_pivot = local[first : first + NB, :]
        own_diag = column[first : first + NB]
        other_pivot, other_diag = (
            partner(own_pivot.astype(jnp.bfloat16), "sub", 0).astype(own_pivot.dtype),
            partner(own_diag.astype(jnp.bfloat16), "sub", 0).astype(own_diag.dtype),
        )
        holder = sibling == step % 2
        pivot_rows = jnp.where(holder, own_pivot, other_pivot)
        diagonal = jnp.where(holder, own_diag, other_diag)
        factor = jnp.linalg.cholesky(diagonal)
        inverse = jax.scipy.linalg.solve_triangular(factor, identity, lower=True)
        left = outer_product(column, inverse, highest)
        right = lax.dot_general(
            pivot_rows,
            inverse,
            (((0,), (1,)), ((), ())),
            precision=highest,
            preferred_element_type=jnp.float32,
        )
        left_live = jnp.where((row_repeat > step)[:, None], left, 0.0)
        right_live = jnp.where((col_repeat > step)[:, None], right, 0.0)
        local = local - outer_product(left_live, right_live, highest)
        is_owner = column_owner == owner
        current = local[:, local_col : local_col + NB]
        new_col = jnp.where(is_owner, jnp.where((row_repeat >= step)[:, None], left, 0.0), current)
        local = lax.dynamic_update_slice(local, new_col, (0, local_col))
    rows_global = my_rows[:, None]
    cols_global = my_cols[None, :]
    cleared = (cols_global < PIV) & (rows_global < cols_global) | (rows_global < PIV) & (
        cols_global >= PIV
    )
    result = jnp.where(cleared, 0.0, local)
    return result.reshape(front_entries.shape)


def solution(mesh):
    return jax.shard_map(
        on_device,
        mesh=mesh,
        in_specs=(P("sub", None, None, "grid", None), P("sub", "grid", None), P("sub", None)),
        out_specs=P("sub", None, None, "grid", None),
        check_vma=False,
    )
```

profile of v0, /device:TPU:0, one launch (start us, length us, event | category | flops | bytes accessed | tf_op | source)
XLA Modules:
  0.0 928.3 jit_solution(12365081881427203168)
XLA Ops:
  8.2 8.1 scatter_custom_fusion
  16.3 17.4 %gather_fusion.1 = s32[3072]{0:T(1024)S(1)} fusion(s32[3072]{0:T(1024)S(1)} %scatter_custom_fusion, s32[3072]{0:T(1024)S(1)} %broadcast_clamp_fusion.1), kind=kCustom, calls=%fused_computation.1 | custom fusion | bytes 36864 | tf_op jit(solution)/shard_map/gather | solution.py:71
  33.8 4.4 fusion
  38.2 18.6 %gather_fusion.2 = bf16[3072,1024]{1,0:T(8,128)(2,1)} fusion(bf16[1024,2048]{0,1:T(8,128)(2,1)} %fusion, s32[3072]{0:T(1024)S(1)} %broadcast_clamp_fusion), kind=kCustom, calls=%fused_computation.2 | custom fusion | bytes 12595200 | tf_op jit(solution)/shard_map/gather | solution.py:73
  56.8 6.9 select_convert_fusion
  63.7 6.3 all-to-all-start
  70.5 8.4 gather_fusion.4
  79.0 62.5 %all-to-all-done = bf16[1024,2,1536]{0,2,1:T(8,128)(2,1)} async-done(((bf16[1024,2,1536]{0,2,1:T(8,128)(2,1)}), bf16[1024,2,1536]{0,2,1:T(8,128)(2,1)}, u32[]{:S(2)}, u32[]{:S(2)}) %all-to-all-start) | async-done | bytes 6291488 | tf_op jit(solution)/shard_map/all_to_all | solution.py:76
  141.5 8.8 convert_bitcast_fusion
  150.3 12.6 %copy.43 = f32[2,1024,1,1536]{3,1,0,2:T(8,128)} copy(f32[2,1024,1,1536]{1,3,0,2:T(8,128)} %convert_bitcast_fusion) | data formatting | bytes 25165824 | tf_op jit(solution)/shard_map/convert_element_type | solution.py:77
  162.9 14.9 %gather_fusion.5 = bf16[1536,1536]{1,0:T(8,128)(2,1)} fusion(f32[2048,1536]{1,0:T(8,128)} %bitcast.198, s32[2048]{0:T(1024)S(1)} %pad_clamp_fusion), kind=kCustom, calls=%fused_computation.5 | custom fusion | bytes 9443328 | tf_op jit(solution)/shard_map/gather | solution.py:31
  177.8 6.6 copy.46
  184.4 5.4 select_convert_fusion.1
  190.6 8.4 gather_fusion
  199.0 8.9 copy.98
  207.9 9.6 %copy.45 = f32[1536,1536]{0,1:T(8,128)} copy(f32[1536,1536]{1,0:T(8,128)} %bitcast.201) | data formatting | bytes 18874368 | tf_op jit(solution)/shard_map/reshape | solution.py:57
  217.7 14.9 %gather_fusion.3 = f32[1536,1536]{1,0:T(8,128)} fusion(f32[2048,1536]{1,0:T(8,128)} %bitcast.199, s32[2048]{0:T(1024)S(1)} %pad_clamp_fusion.2), kind=kCustom, calls=%fused_computation.3 | custom fusion | bytes 18880512 | tf_op jit(solution)/shard_map/gather | solution.py:31
  232.6 9.6 %copy.44 = f32[1536,1536]{0,1:T(8,128)} copy(f32[1536,1536]{1,0:T(8,128)} %gather_fusion.3) | data formatting | bytes 18874368 | tf_op jit(solution)/shard_map/gather | solution.py:31
  242.3 8.6 convert_subtract_fusion
  250.9 3.7 copy-done.3
  256.4 34.3 %all-reduce.9.cloned.1.call-done = f32[1536,128]{0,1:T(8,128)} async-done(((f32[1536,128]{0,1:T(8,128)}), f32[1536,128]{0,1:T(8,128)}) %all-reduce.9.cloned.1.call-update) | async-done | bytes 786448 | tf_op jit(solution)/shard_map/psum | solution.py:17
  294.3 11.7 %cholesky.134 = f32[128,128]{1,0:T(8,128)S(1)} custom-call(f32[128,128]{1,0:T(8,128)S(1)} %fusion.106), custom_call_target="Cholesky" | custom-call | tf_op jit(solution)/shard_map/jit(cholesky)/cholesky | solution.py:103
  307.4 9.8 %custom-call.12 = f32[1,128,128]{1,2,0:T(8,128)S(1)} custom-call(f32[1,128,128]{2,1,0:T(8,128)S(1)} %fusion.83), custom_call_target="InvertDiagBlocksLowerTriangular" | custom-call | tf_op jit(solution)/shard_map/jit(_solve_triangular)/triangular_solve | solution.py:104
  321.6 11.9 %convolution_subtract_fusion.7 = f32[1536,1536]{0,1:T(8,128)} fusion(f32[1536,1536]{0,1:T(8,128)} %copy-done.3, f32[1536,128]{0,1:T(8,128)S(1)} %convolution_select_fusion.7, f32[1536,128]{0,1:T(8,128)S(1)} %fusion.125, pred[1536]{0:T(1024)(128)(4,1)S(1)} %broadcast_bitcast_fusion.23), kind=kOutput, calls=%fused_computation.16 | convolution fusion | flops 3626434560 | bytes 20448768 | tf_op jit(solution)/shard_map/dot_general | solution.py:36
  333.5 2.5 broadcast_select_fusion.3
  336.5 34.1 %all-reduce.11.cloned.1.call-done = f32[1536,128]{0,1:T(8,128)} async-done(((f32[1536,128]{0,1:T(8,128)}), f32[1536,128]{0,1:T(8,128)}) %all-reduce.11.cloned.1.call-update) | async-done | bytes 786448 | tf_op jit(solution)/shard_map/psum | solution.py:17
  374.1 11.7 %cholesky.145 = f32[128,128]{1,0:T(8,128)S(1)} custom-call(f32[128,128]{1,0:T(8,128)S(1)} %fusion.104), custom_call_target="Cholesky" | custom-call | tf_op jit(solution)/shard_map/jit(cholesky)/cholesky | solution.py:103
  387.2 9.8 %custom-call.13 = f32[1,128,128]{1,2,0:T(8,128)S(1)} custom-call(f32[1,128,128]{2,1,0:T(8,128)S(1)} %fusion.84), custom_call_target="InvertDiagBlocksLowerTriangular" | custom-call | tf_op jit(solution)/shard_map/jit(_solve_triangular)/triangular_solve | solution.py:104
  401.4 10.6 %convolution_subtract_fusion.6 = f32[1536,1536]{0,1:T(8,128)S(1)} fusion(f32[1536,1536]{0,1:T(8,128)} %get-tuple-element.14, f32[1536,128]{0,1:T(8,128)S(1)} %convolution_select_fusion.6, f32[1536,128]{0,1:T(8,128)S(1)} %fusion.126, pred[1536]{0:T(1024)(128)(4,1)S(1)} %broadcast_bitcast_fusion.20), kind=kOutput, calls=%fused_computation.15 | convolution fusion | flops 3626434560 | bytes 20448768 | tf_op jit(solution)/shard_map/dot_general | solution.py:36
  412.2 3.7 copy-done
  417.6 33.8 %all-reduce.13.cloned.1.call-done = f32[1536,128]{0,1:T(8,128)} async-done(((f32[1536,128]{0,1:T(8,128)}), f32[1536,128]{0,1:T(8,128)}) %all-reduce.13.cloned.1.call-update) | async-done | bytes 786448 | tf_op jit(solution)/shard_map/psum | solution.py:17
  455.0 11.7 %cholesky.156 = f32[128,128]{1,0:T(8,128)S(1)} custom-call(f32[128,128]{1,0:T(8,128)S(1)} %fusion.102), custom_call_target="Cholesky" | custom-call | tf_op jit(solution)/shard_map/jit(cholesky)/cholesky | solution.py:103
  468.1 9.8 %custom-call.14 = f32[1,128,128]{1,2,0:T(8,128)S(1)} custom-call(f32[1,128,128]{2,1,0:T(8,128)S(1)} %fusion.85), custom_call_target="InvertDiagBlocksLowerTriangular" | custom-call | tf_op jit(solution)/shard_map/jit(_solve_triangular)/triangular_solve | solution.py:104
  482.3 11.9 %convolution_subtract_fusion.5 = f32[1536,1536]{0,1:T(8,128)} fusion(f32[1536,1536]{0,1:T(8,128)} %copy-done, f32[1536,128]{0,1:T(8,128)S(1)} %convolution_select_fusion.5, f32[1536,128]{0,1:T(8,128)S(1)} %fusion.127, pred[1536]{0:T(1024)(128)(4,1)S(1)} %broadcast_bitcast_fusion.17), kind=kOutput, calls=%fused_computation.14 | convolution fusion | flops 3626434560 | bytes 20448768 | tf_op jit(solution)/shard_map/dot_general | solution.py:36
  494.2 2.5 broadcast_select_fusion.2
  497.1 34.1 %all-reduce.15.cloned.1.call-done = f32[1536,128]{0,1:T(8,128)} async-done(((f32[1536,128]{0,1:T(8,128)}), f32[1536,128]{0,1:T(8,128)}) %all-reduce.15.cloned.1.call-update) | async-done | bytes 786448 | tf_op jit(solution)/shard_map/psum | solution.py:17
  534.8 11.7 %cholesky.167 = f32[128,128]{1,0:T(8,128)S(1)} custom-call(f32[128,128]{1,0:T(8,128)S(1)} %fusion.100), custom_call_target="Cholesky" | custom-call | tf_op jit(solution)/shard_map/jit(cholesky)/cholesky | solution.py:103
  547.9 9.8 %custom-call.15 = f32[1,128,128]{1,2,0:T(8,128)S(1)} custom-call(f32[1,128,128]{2,1,0:T(8,128)S(1)} %fusion.86), custom_call_target="InvertDiagBlocksLowerTriangular" | custom-call | tf_op jit(solution)/shard_map/jit(_solve_triangular)/triangular_solve | solution.py:104
  562.1 10.6 %convolution_subtract_fusion.4 = f32[1536,1536]{0,1:T(8,128)S(1)} fusion(f32[1536,1536]{0,1:T(8,128)} %get-tuple-element.12, f32[1536,128]{0,1:T(8,128)S(1)} %convolution_select_fusion.4, f32[1536,128]{0,1:T(8,128)S(1)} %fusion.128, pred[1536]{0:T(1024)(128)(4,1)S(1)} %broadcast_bitcast_fusion.14), kind=kOutput, calls=%fused_computation.13 | convolution fusion | flops 3626434560 | bytes 20448768 | tf_op jit(solution)/shard_map/dot_general | solution.py:36
  572.9 3.7 copy-done.1
  578.3 33.8 %all-reduce.17.cloned.1.call-done = f32[1536,128]{0,1:T(8,128)} async-done(((f32[1536,128]{0,1:T(8,128)}), f32[1536,128]{0,1:T(8,128)}) %all-reduce.17.cloned.1.call-update) | async-done | bytes 786448 | tf_op jit(solution)/shard_map/psum | solution.py:17
  615.7 11.7 %cholesky.178 = f32[128,128]{1,0:T(8,128)S(1)} custom-call(f32[128,128]{1,0:T(8,128)S(1)} %fusion.98), custom_call_target="Cholesky" | custom-call | tf_op jit(solution)/shard_map/jit(cholesky)/cholesky | solution.py:103
  628.8 9.8 %custom-call.16 = f32[1,128,128]{1,2,0:T(8,128)S(1)} custom-call(f32[1,128,128]{2,1,0:T(8,128)S(1)} %fusion.87), custom_call_target="InvertDiagBlocksLowerTriangular" | custom-call | tf_op jit(solution)/shard_map/jit(_solve_triangular)/triangular_solve | solution.py:104
  640.9 2.0 convolution_select_fusion.3
  642.9 11.9 %convolution_subtract_fusion.3 = f32[1536,1536]{0,1:T(8,128)} fusion(f32[1536,1536]{0,1:T(8,128)} %copy-done.1, f32[1536,128]{0,1:T(8,128)S(1)} %convolution_select_fusion.3, f32[1536,128]{0,1:T(8,128)S(1)} %fusion.129, pred[1536]{0:T(1024)(128)(4,1)S(1)} %broadcast_bitcast_fusion.11), kind=kOutput, calls=%fused_computation.12 | convolution fusion | flops 3626434560 | bytes 20448768 | tf_op jit(solution)/shard_map/dot_general | solution.py:36
  654.8 2.5 broadcast_select_fusion.1
  657.8 34.1 %all-reduce.19.cloned.1.call-done = f32[1536,128]{0,1:T(8,128)} async-done(((f32[1536,128]{0,1:T(8,128)}), f32[1536,128]{0,1:T(8,128)}) %all-reduce.19.cloned.1.call-update) | async-done | bytes 786448 | tf_op jit(solution)/shard_map/psum | solution.py:17
  695.5 11.7 %cholesky.189 = f32[128,128]{1,0:T(8,128)S(1)} custom-call(f32[128,128]{1,0:T(8,128)S(1)} %fusion.96), custom_call_target="Cholesky" | custom-call | tf_op jit(solution)/shard_map/jit(cholesky)/cholesky | solution.py:103
  708.6 9.8 %custom-call.17 = f32[1,128,128]{1,2,0:T(8,128)S(1)} custom-call(f32[1,128,128]{2,1,0:T(8,128)S(1)} %fusion.88), custom_call_target="InvertDiagBlocksLowerTriangular" | custom-call | tf_op jit(solution)/shard_map/jit(_solve_triangular)/triangular_solve | solution.py:104
  722.7 10.6 %convolution_subtract_fusion.2 = f32[1536,1536]{0,1:T(8,128)S(1)} fusion(f32[1536,1536]{0,1:T(8,128)} %get-tuple-element.10, f32[1536,128]{0,1:T(8,128)S(1)} %convolution_select_fusion.2, f32[1536,128]{0,1:T(8,128)S(1)} %fusion.130, pred[1536]{0:T(1024)(128)(4,1)S(1)} %broadcast_bitcast_fusion.8), kind=kOutput, calls=%fused_computation.11 | convolution fusion | flops 3626434560 | bytes 20448768 | tf_op jit(solution)/shard_map/dot_general | solution.py:36
  733.5 3.7 copy-done.2
  738.8 34.0 %all-reduce.21.cloned.1.call-done = f32[1536,128]{0,1:T(8,128)} async-done(((f32[1536,128]{0,1:T(8,128)}), f32[1536,128]{0,1:T(8,128)}) %all-reduce.21.cloned.1.call-update) | async-done | bytes 786448 | tf_op jit(solution)/shard_map/psum | solution.py:17
  776.4 11.7 %cholesky.200 = f32[128,128]{1,0:T(8,128)S(1)} custom-call(f32[128,128]{1,0:T(8,128)S(1)} %fusion.94), custom_call_target="Cholesky" | custom-call | tf_op jit(solution)/shard_map/jit(cholesky)/cholesky | solution.py:103
  789.5 9.8 %custom-call.18 = f32[1,128,128]{1,2,0:T(8,128)S(1)} custom-call(f32[1,128,128]{2,1,0:T(8,128)S(1)} %fusion.89), custom_call_target="InvertDiagBlocksLowerTriangular" | custom-call | tf_op jit(solution)/shard_map/jit(_solve_triangular)/triangular_solve | solution.py:104
  803.6 12.3 %convolution_subtract_fusion.1 = f32[1536,1536]{0,1:T(8,128)} fusion(f32[1536,1536]{0,1:T(8,128)} %copy-done.2, f32[1536,128]{0,1:T(8,128)S(1)} %convolution_select_fusion.1, f32[1536,128]{0,1:T(8,128)S(1)} %fusion.131, pred[1536]{0:T(1024)(128)(4,1)S(1)} %broadcast_bitcast_fusion.5), kind=kOutput, calls=%fused_computation.10 | convolution fusion | flops 3626434560 | bytes 20448768 | tf_op jit(solution)/shard_map/dot_general | solution.py:36
  815.9 2.5 broadcast_select_fusion
  818.7 34.3 %all-reduce.23.cloned.1.call-done = f32[1536,128]{0,1:T(8,128)} async-done(((f32[1536,128]{0,1:T(8,128)}), f32[1536,128]{0,1:T(8,128)}) %all-reduce.23.cloned.1.call-update) | async-done | bytes 786448 | tf_op jit(solution)/shard_map/psum | solution.py:17
  856.6 11.7 %cholesky.211 = f32[128,128]{1,0:T(8,128)S(1)} custom-call(f32[128,128]{1,0:T(8,128)S(1)} %fusion.92), custom_call_target="Cholesky" | custom-call | tf_op jit(solution)/shard_map/jit(cholesky)/cholesky | solution.py:103
  869.7 9.8 %custom-call.19 = f32[1,128,128]{1,2,0:T(8,128)S(1)} custom-call(f32[1,128,128]{2,1,0:T(8,128)S(1)} %fusion.90), custom_call_target="InvertDiagBlocksLowerTriangular" | custom-call | tf_op jit(solution)/shard_map/jit(_solve_triangular)/triangular_solve | solution.py:104
  881.8 2.0 convolution_select_fusion
  883.8 10.8 %convolution_subtract_fusion = f32[1536,1536]{0,1:T(8,128)S(1)} fusion(f32[1536,1536]{0,1:T(8,128)} %get-tuple-element.8, f32[1536,128]{0,1:T(8,128)S(1)} %convolution_select_fusion, f32[1536,128]{0,1:T(8,128)S(1)} %fusion.132, pred[1536]{0:T(1024)(128)(4,1)S(1)} %broadcast_bitcast_fusion.2), kind=kOutput, calls=%fused_computation.9 | convolution fusion | flops 3626434560 | bytes 20448768 | tf_op jit(solution)/shard_map/dot_general | solution.py:36
  894.8 5.1 or_select_fusion
  899.9 9.6 %copy.79 = f32[1536,1536]{1,0:T(8,128)} copy(f32[1536,1536]{0,1:T(8,128)} %or_select_fusion) | data formatting | bytes 18874368 | tf_op jit(solution)/shard_map/jit(_where)/select_n | solution.py:125
  909.6 12.0 %copy.80 = f32[1,12,128,1,1536]{4,3,2,1,0:T(1,128)} copy(f32[1,12,128,1,1536]{4,2,1,3,0:T(8,128)} %bitcast.200) | data formatting | bytes 18874368 | tf_op jit(solution)/shard_map/reshape | solution.py:126
  (231 shorter events, 81.9 us)
Async XLA Ops:
  6.5 27.2 %copy-start.4 = (bf16[1,1024,256]{2,1,0:T(8,128)(2,1)S(1)}, bf16[1,1024,256]{2,1,0:T(8,128)(2,1)}, u32[]{:S(2)}) copy-start(bf16[1,1024,256]{2,1,0:T(8,128)(2,1)} %param.7) | copy-start | bytes 1572868
  6.5 27.2 %all-gather.2.cloned.1.call-start = ((), (), s32[]{:S(2)}) async-start(), calls=%async_computation.1 | async-start | bytes 1572864 | tf_op jit(solution)/shard_map/all_gather | solution.py:64
  63.7 77.7 %all-to-all-start = ((bf16[1024,2,1536]{0,2,1:T(8,128)(2,1)}), bf16[1024,2,1536]{0,2,1:T(8,128)(2,1)}, u32[]{:S(2)}, u32[]{:S(2)}) async-start(bf16[1024,2,1536]{0,2,1:T(8,128)(2,1)} %select_convert_fusion), calls=%async_computation | async-start | bytes 12582912 | tf_op jit(solution)/shard_map/all_to_all | solution.py:76
  70.0 220.7 %all-reduce.9.cloned.1.call-start = ((), (), s32[]{:S(2)}) async-start(), calls=%async_computation.2 | async-start | bytes 1572864 | tf_op jit(solution)/shard_map/psum | solution.py:17
  189.9 52.4 %collective-permute-start = (bf16[1536,1536]{0,1:T(8,128)(2,1)}, bf16[1536,1536]{0,1:T(8,128)(2,1)}, u32[]{:S(2)}, u32[]{:S(2)}) collective-permute-start(bf16[1536,1536]{0,1:T(8,128)(2,1)} %select_convert_fusion.1), channel_id=1, source_target_pairs={{0,2},{2,0},{4,6},{6,4},{8,10},{10,8},{12,14},{14,12},{16,18},{18,... | collective-permute-start | bytes 14155784 | tf_op jit(solution)/shard_map/ppermute | solution.py:12
  250.9 3.7 copy-start.3
  255.6 115.0 %all-reduce.11.cloned.1.call-start = ((), (), s32[]{:S(2)}) async-start(), calls=%async_computation.3 | async-start | bytes 1572864 | tf_op jit(solution)/shard_map/psum | solution.py:17
  291.6 1.8 collective-permute-start.1
  292.8 26.7 %collective-permute-start.2 = (bf16[128,1536]{0,1:T(8,128)(2,1)S(1)}, bf16[128,1536]{0,1:T(8,128)(2,1)S(1)}, u32[]{:S(2)}, u32[]{:S(2)}) collective-permute-start(bf16[128,1536]{0,1:T(8,128)(2,1)S(1)} %slice.263), channel_id=1, source_target_pairs={{0,2},{2,0},{4,6},{6,4},{8,10},{10,8},{12,14},{14,12},{16,18},{18,... | collective-permute-start | bytes 1179656 | tf_op jit(solution)/shard_map/ppermute | solution.py:12
  336.0 115.5 %all-reduce.13.cloned.1.call-start = ((), (), s32[]{:S(2)}) async-start(), calls=%async_computation.4 | async-start | bytes 1572864 | tf_op jit(solution)/shard_map/psum | solution.py:17
  371.4 1.8 collective-permute-start.3
  372.6 26.7 %collective-permute-start.4 = (bf16[128,1536]{0,1:T(8,128)(2,1)S(1)}, bf16[128,1536]{0,1:T(8,128)(2,1)S(1)}, u32[]{:S(2)}, u32[]{:S(2)}) collective-permute-start(bf16[128,1536]{0,1:T(8,128)(2,1)S(1)} %slice.262), channel_id=1, source_target_pairs={{0,2},{2,0},{4,6},{6,4},{8,10},{10,8},{12,14},{14,12},{16,18},{18,... | collective-permute-start | bytes 1179656 | tf_op jit(solution)/shard_map/ppermute | solution.py:12
  412.2 3.7 copy-start
  416.9 114.3 %all-reduce.15.cloned.1.call-start = ((), (), s32[]{:S(2)}) async-start(), calls=%async_computation.5 | async-start | bytes 1572864 | tf_op jit(solution)/shard_map/psum | solution.py:17
  452.3 1.8 collective-permute-start.5
  453.5 26.7 %collective-permute-start.6 = (bf16[128,1536]{0,1:T(8,128)(2,1)S(1)}, bf16[128,1536]{0,1:T(8,128)(2,1)S(1)}, u32[]{:S(2)}, u32[]{:S(2)}) collective-permute-start(bf16[128,1536]{0,1:T(8,128)(2,1)S(1)} %slice.261), channel_id=1, source_target_pairs={{0,2},{2,0},{4,6},{6,4},{8,10},{10,8},{12,14},{14,12},{16,18},{18,... | collective-permute-start | bytes 1179656 | tf_op jit(solution)/shard_map/ppermute | solution.py:12
  496.7 115.4 %all-reduce.17.cloned.1.call-start = ((), (), s32[]{:S(2)}) async-start(), calls=%async_computation.6 | async-start | bytes 1572864 | tf_op jit(solution)/shard_map/psum | solution.py:17
  532.1 1.8 collective-permute-start.7
  533.3 26.7 %collective-permute-start.8 = (bf16[128,1536]{0,1:T(8,128)(2,1)S(1)}, bf16[128,1536]{0,1:T(8,128)(2,1)S(1)}, u32[]{:S(2)}, u32[]{:S(2)}) collective-permute-start(bf16[128,1536]{0,1:T(8,128)(2,1)S(1)} %slice.260), channel_id=1, source_target_pairs={{0,2},{2,0},{4,6},{6,4},{8,10},{10,8},{12,14},{14,12},{16,18},{18,... | collective-permute-start | bytes 1179656 | tf_op jit(solution)/shard_map/ppermute | solution.py:12
  572.9 3.7 copy-start.1
  577.6 114.3 %all-reduce.19.cloned.1.call-start = ((), (), s32[]{:S(2)}) async-start(), calls=%async_computation.7 | async-start | bytes 1572864 | tf_op jit(solution)/shard_map/psum | solution.py:17
  613.0 1.8 collective-permute-start.9
  614.2 26.7 %collective-permute-start.10 = (bf16[128,1536]{0,1:T(8,128)(2,1)S(1)}, bf16[128,1536]{0,1:T(8,128)(2,1)S(1)}, u32[]{:S(2)}, u32[]{:S(2)}) collective-permute-start(bf16[128,1536]{0,1:T(8,128)(2,1)S(1)} %slice.259), channel_id=1, source_target_pairs={{0,2},{2,0},{4,6},{6,4},{8,10},{10,8},{12,14},{14,12},{16,18},{18,... | collective-permute-start | bytes 1179656 | tf_op jit(solution)/shard_map/ppermute | solution.py:12
  657.3 115.5 %all-reduce.21.cloned.1.call-start = ((), (), s32[]{:S(2)}) async-start(), calls=%async_computation.8 | async-start | bytes 1572864 | tf_op jit(solution)/shard_map/psum | solution.py:17
  692.8 1.8 collective-permute-start.11
  694.0 26.7 %collective-permute-start.12 = (bf16[128,1536]{0,1:T(8,128)(2,1)S(1)}, bf16[128,1536]{0,1:T(8,128)(2,1)S(1)}, u32[]{:S(2)}, u32[]{:S(2)}) collective-permute-start(bf16[128,1536]{0,1:T(8,128)(2,1)S(1)} %slice.258), channel_id=1, source_target_pairs={{0,2},{2,0},{4,6},{6,4},{8,10},{10,8},{12,14},{14,12},{16,18},{18,... | collective-permute-start | bytes 1179656 | tf_op jit(solution)/shard_map/ppermute | solution.py:12
  733.5 3.7 copy-start.2
  738.3 114.7 %all-reduce.23.cloned.1.call-start = ((), (), s32[]{:S(2)}) async-start(), calls=%async_computation.9 | async-start | bytes 1572864 | tf_op jit(solution)/shard_map/psum | solution.py:17
  773.6 1.8 collective-permute-start.13
  774.8 26.7 %collective-permute-start.14 = (bf16[128,1536]{0,1:T(8,128)(2,1)S(1)}, bf16[128,1536]{0,1:T(8,128)(2,1)S(1)}, u32[]{:S(2)}, u32[]{:S(2)}) collective-permute-start(bf16[128,1536]{0,1:T(8,128)(2,1)S(1)} %slice.257), channel_id=1, source_target_pairs={{0,2},{2,0},{4,6},{6,4},{8,10},{10,8},{12,14},{14,12},{16,18},{18,... | collective-permute-start | bytes 1179656 | tf_op jit(solution)/shard_map/ppermute | solution.py:12
  853.8 1.8 collective-permute-start.15
  855.0 26.7 %collective-permute-start.16 = (bf16[128,1536]{0,1:T(8,128)(2,1)S(1)}, bf16[128,1536]{0,1:T(8,128)(2,1)S(1)}, u32[]{:S(2)}, u32[]{:S(2)}) collective-permute-start(bf16[128,1536]{0,1:T(8,128)(2,1)S(1)} %slice.256), channel_id=1, source_target_pairs={{0,2},{2,0},{4,6},{6,4},{8,10},{10,8},{12,14},{14,12},{16,18},{18,... | collective-permute-start | bytes 1179656 | tf_op jit(solution)/shard_map/ppermute | solution.py:12
  883.8 11.0 %copy-start.5 = (s32[1536]{0:T(1024)S(1)}, s32[1536]{0:T(1024)}, u32[]{:S(2)}) copy-start(s32[1536]{0:T(1024)} %get-tuple-element.17) | copy-start | bytes 18436
Sparse Core Ops, SparseCore 0:
  8.9 23.9 all-gather.1
  255.7 34.9 all-reduce.8
  336.1 34.4 all-reduce.10
  417.0 34.3 all-reduce.12
  496.8 34.4 all-reduce.14
  577.7 34.3 all-reduce.16
  657.5 34.4 all-reduce.18
  738.4 34.3 all-reduce.20
  818.5 34.3 all-reduce.22
where the time goes:
time: 936 us; the launch traced here: 928 us
  waiting for transfers between devices  336 us (36%)
  other arithmetic  242 us (26%)
  local copies, waits for them, and re-layouts  193 us (21%)
  matrix products  129 us (14%)
  between operations  14.4 us (2%)
  starting transfers between devices  13.6 us (1%)
    psum x8, waiting for transfers between devices, broadcast(): return lax.psum(jnp.where(mine, shard, jnp.zeros_like(shard)), axis)  273 us
    dot_general x17, matrix products, outer_product(): lax.dot_general(left, right, (((1,), (1,)), ((), ())), precision=precisio...  111 us
    another operation x24, other arithmetic, on_device(): factor = jnp.linalg.cholesky(diagonal)  99.6 us
    another operation x16, other arithmetic, on_device(): inverse = jax.scipy.linalg.solve_triangular(factor, identity, lower=True)  83.6 us
    all_to_all x1, waiting for transfers between devices, on_device(): lax.all_to_all(spread.astype(jnp.bfloat16), 'grid', split_axis=1, concat_...  62.5 us
    gather x4, local copies, waits for them, and re-layouts, select_rows(): picked = table[jnp.where(found, index, 0)]  46.1 us
    unnamed x13, local copies, waits for them, and re-layouts  23.9 us
  transfers between devices with their start and end apart: 27, of which 9 were waited for; matrix products, arithmetic and copies ran while one was open for 33% of the time, Pallas kernels for 0%

commit v1 on v0

--- a/solution.py
+++ b/solution.py
@@ -14,7 +14,7 @@
 
 def broadcast(shard, axis, root):
     mine = lax.axis_index(axis) == root
-    return lax.psum(jnp.where(mine, shard, jnp.zeros_like(shard)), axis)
+    return jnp.sum(lax.all_gather(jnp.where(mine, shard, jnp.zeros_like(shard)), axis), axis=0)
 
 
 def invert_map(mapping):

time: 936 us -> 836 us (0.89)
  waiting for transfers between devices: 336 us -> 279 us
  local copies, waits for them, and re-layouts: 193 us -> 151 us
    psum x8 -> x0, waiting for transfers between devices: 273 us -> none  [broadcast(): return lax.psum(jnp.where(mine, shard, jnp.zeros_like(shard)), axis)]
    all_gather x0 -> x8, waiting for transfers between devices: none -> 215 us  [broadcast(): lax.all_gather(jnp.where(mine, shard, jnp.zeros_like(shard)), axis)]
    gather x4 -> x2, local copies, waits for them, and re-layouts: 46.1 us -> 29.9 us  [select_rows(): picked = table[jnp.where(found, index, 0)]]
    reduce_sum x0 -> x8, other arithmetic: none -> 12.7 us  [broadcast(): jnp.sum(lax.all_gather(jnp.where(mine, shard, jnp.zeros_like(shard)), axi...]
    select_n x1 -> x0, local copies, waits for them, and re-layouts: 9.63 us -> none  [on_device(): result = jnp.where(cleared, 0.0, local)]
    reshape x1 -> x0, local copies, waits for them, and re-layouts: 9.61 us -> none  [on_device(): local = front_entries.reshape(row_blocks * NB, col_width)]
    unnamed x13 -> x19, local copies, waits for them, and re-layouts: 23.9 us -> 24.6 us
where the time goes in v1:
time: 836 us; the launch traced here: 830 us
  waiting for transfers between devices  279 us (33%)
  other arithmetic  247 us (30%)
  local copies, waits for them, and re-layouts  151 us (18%)
  matrix products  125 us (15%)
  between operations  14.7 us (2%)
  starting transfers between devices  14.1 us (2%)
    all_gather x8, waiting for transfers between devices, broadcast(): lax.all_gather(jnp.where(mine, shard, jnp.zeros_like(shard)), axis)  215 us
    dot_general x17, matrix products, outer_product(): lax.dot_general(left, right, (((1,), (1,)), ((), ())), precision=precisio...  102 us
    another operation x24, other arithmetic, on_device(): factor = jnp.linalg.cholesky(diagonal)  99.7 us
    another operation x16, other arithmetic, on_device(): inverse = jax.scipy.linalg.solve_triangular(factor, identity, lower=True)  84.1 us
    all_to_all x1, waiting for transfers between devices, on_device(): lax.all_to_all(spread.astype(jnp.bfloat16), 'grid', split_axis=1, concat_...  62.5 us
    gather x2, local copies, waits for them, and re-layouts, select_rows(): picked = table[jnp.where(found, index, 0)]  29.9 us
    unnamed x19, local copies, waits for them, and re-layouts  24.6 us
    dot_general x8, matrix products, on_device(): lax.dot_general(pivot_rows, inverse, (((0,), (1,)), ((), ())), precision=...  21.2 us
  transfers between devices with their start and end apart: 27, of which 9 were waited for; matrix products, arithmetic and copies ran while one was open for 33% of the time, Pallas kernels for 0%

profile of v1, /device:TPU:0, one launch (start us, length us, event | category | flops | bytes accessed | tf_op | source)
XLA Modules:
  0.0 830.4 jit_solution(10001268191058713503)
XLA Ops:
  8.2 8.1 scatter_custom_fusion
  16.3 17.4 %gather_fusion.1 = s32[3072]{0:T(1024)S(1)} fusion(s32[3072]{0:T(1024)S(1)} %scatter_custom_fusion, s32[3072]{0:T(1024)S(1)} %broadcast_clamp_fusion.1), kind=kCustom, calls=%fused_computation.1 | custom fusion | bytes 36864 | tf_op jit(solution)/shard_map/gather | solution.py:71
  33.8 4.4 fusion.1
  38.2 18.6 %gather_fusion.2 = bf16[3072,1024]{1,0:T(8,128)(2,1)} fusion(bf16[1024,2048]{0,1:T(8,128)(2,1)} %fusion.1, s32[3072]{0:T(1024)S(1)} %broadcast_clamp_fusion), kind=kCustom, calls=%fused_computation.2 | custom fusion | bytes 12595200 | tf_op jit(solution)/shard_map/gather | solution.py:73
  56.8 6.9 select_convert_fusion
  63.7 6.3 all-to-all-start
  70.5 8.4 %gather_fusion.4 = s32[1536]{0:T(1024)S(1)} fusion(s32[3072]{0:T(1024)S(1)} %scatter_custom_fusion, s32[2048]{0:T(1024)S(1)} %pad_clamp_fusion.1), kind=kCustom, calls=%fused_computation.4 | custom fusion | bytes 18432 | tf_op jit(solution)/shard_map/gather | solution.py:29
  79.0 62.5 %all-to-all-done = bf16[1024,2,1536]{0,2,1:T(8,128)(2,1)} async-done(((bf16[1024,2,1536]{0,2,1:T(8,128)(2,1)}), bf16[1024,2,1536]{0,2,1:T(8,128)(2,1)}, u32[]{:S(2)}, u32[]{:S(2)}) %all-to-all-start) | async-done | bytes 6291488 | tf_op jit(solution)/shard_map/all_to_all | solution.py:76
  141.5 8.8 %convert_bitcast_fusion = f32[2,1024,1,1536]{1,3,0,2:T(8,128)} fusion(bf16[1024,2,1536]{0,2,1:T(8,128)(2,1)} %all-to-all-done), kind=kLoop, calls=%fused_computation.7 | loop fusion | flops 3145728 | bytes 18874368 | tf_op jit(solution)/shard_map/convert_element_type | solution.py:77
  150.3 12.6 %copy.27 = f32[2,1024,1,1536]{3,1,0,2:T(8,128)} copy(f32[2,1024,1,1536]{1,3,0,2:T(8,128)} %convert_bitcast_fusion) | data formatting | bytes 25165824 | tf_op jit(solution)/shard_map/convert_element_type | solution.py:77
  162.9 14.9 %gather_fusion.5 = bf16[1536,1536]{1,0:T(8,128)(2,1)} fusion(f32[2048,1536]{1,0:T(8,128)} %bitcast.209, s32[2048]{0:T(1024)S(1)} %pad_clamp_fusion), kind=kCustom, calls=%fused_computation.5 | custom fusion | bytes 9443328 | tf_op jit(solution)/shard_map/gather | solution.py:31
  177.8 5.4 select_convert_fusion.1
  183.3 8.4 %gather_fusion = s32[1536]{0:T(1024)S(1)} fusion(s32[3072]{0:T(1024)S(1)} %scatter_custom_fusion, s32[2048]{0:T(1024)S(1)} %pad_clamp_fusion.3), kind=kCustom, calls=%fused_computation | custom fusion | bytes 18432 | tf_op jit(solution)/shard_map/gather | solution.py:29
  191.7 8.9 %copy.46 = f32[1,12,128,1,1536]{4,2,3,1,0:T(8,128)} copy(f32[1,12,128,1,1536]{4,3,2,1,0:T(1,128)} %param.6) | data formatting | bytes 18874368
  200.7 14.9 %gather_fusion.3 = f32[1536,1536]{1,0:T(8,128)} fusion(f32[2048,1536]{1,0:T(8,128)} %bitcast.210, s32[2048]{0:T(1024)S(1)} %pad_clamp_fusion.2), kind=kCustom, calls=%fused_computation.3 | custom fusion | bytes 18880512 | tf_op jit(solution)/shard_map/gather | solution.py:31
  215.6 8.7 %fusion = f32[1536,1536]{1,0:T(8,128)S(1)} fusion(f32[1,12,128,1,1536]{4,2,3,1,0:T(8,128)} %copy.46, bf16[1536,1536]{1,0:T(8,128)(2,1)} %collective-permute-done, f32[1536,1536]{1,0:T(8,128)} %gather_fusion.3, pred[1536]{0:T(1024)(128)(4,1)S(1)} %broadcast_compare_fusion.2), kind=kLoop, calls=%fused_computation.18 | loop fusion | flops 9437184 | bytes 33031680 | tf_op jit(solution)/shard_map/sub | solution.py:84
  224.4 3.7 copy-done.3
  229.9 27.2 %all-gather.20.cloned.1.call-done = f32[3072,128]{1,0:T(8,128)} async-done(((f32[1536,128]{1,0:T(8,128)}), f32[3072,128]{1,0:T(8,128)}) %all-gather.20.cloned.1.call-update) | async-done | bytes 1572880 | tf_op jit(solution)/shard_map/all_gather | solution.py:17
  260.8 11.7 %cholesky.134 = f32[128,128]{1,0:T(8,128)S(1)} custom-call(f32[128,128]{1,0:T(8,128)S(1)} %fusion.107), custom_call_target="Cholesky" | custom-call | tf_op jit(solution)/shard_map/jit(cholesky)/cholesky | solution.py:103
  274.0 9.8 %custom-call.12 = f32[1,128,128]{1,2,0:T(8,128)S(1)} custom-call(f32[1,128,128]{2,1,0:T(8,128)S(1)} %fusion.84), custom_call_target="InvertDiagBlocksLowerTriangular" | custom-call | tf_op jit(solution)/shard_map/jit(_solve_triangular)/triangular_solve | solution.py:104
  284.9 2.6 convolution_select_fusion.7
  287.6 11.9 %convolution_subtract_fusion.7 = f32[1536,1536]{1,0:T(8,128)} fusion(f32[1536,1536]{1,0:T(8,128)} %copy-done.3, f32[1536,128]{1,0:T(8,128)S(1)} %convolution_select_fusion.7, f32[1536,128]{1,0:T(8,128)S(1)} %fusion.126, pred[1536]{0:T(1024)(128)(4,1)S(1)} %broadcast_bitcast_fusion.23), kind=kOutput, calls=%fused_computation.16 | convolution fusion | flops 3626434560 | bytes 20448768 | tf_op jit(solution)/shard_map/dot_general | solution.py:36
  299.5 2.6 broadcast_select_fusion.3
  302.5 26.9 %all-gather.22.cloned.1.call-done = f32[3072,128]{1,0:T(8,128)} async-done(((f32[1536,128]{1,0:T(8,128)}), f32[3072,128]{1,0:T(8,128)}) %all-gather.22.cloned.1.call-update) | async-done | bytes 1572880 | tf_op jit(solution)/shard_map/all_gather | solution.py:17
  333.1 11.7 %cholesky.145 = f32[128,128]{1,0:T(8,128)S(1)} custom-call(f32[128,128]{1,0:T(8,128)S(1)} %fusion.105), custom_call_target="Cholesky" | custom-call | tf_op jit(solution)/shard_map/jit(cholesky)/cholesky | solution.py:103
  346.3 9.8 %custom-call.13 = f32[1,128,128]{1,2,0:T(8,128)S(1)} custom-call(f32[1,128,128]{2,1,0:T(8,128)S(1)} %fusion.85), custom_call_target="InvertDiagBlocksLowerTriangular" | custom-call | tf_op jit(solution)/shard_map/jit(_solve_triangular)/triangular_solve | solution.py:104
  357.2 2.6 convolution_select_fusion.6
  359.9 10.7 %convolution_subtract_fusion.6 = f32[1536,1536]{1,0:T(8,128)S(1)} fusion(f32[1536,1536]{1,0:T(8,128)} %get-tuple-element.14, f32[1536,128]{1,0:T(8,128)S(1)} %convolution_select_fusion.6, f32[1536,128]{1,0:T(8,128)S(1)} %fusion.127, pred[1536]{0:T(1024)(128)(4,1)S(1)} %broadcast_bitcast_fusion.20), kind=kOutput, calls=%fused_computation.15 | convolution fusion | flops 3626434560 | bytes 20448768 | tf_op jit(solution)/shard_map/dot_general | solution.py:36
  371.0 3.7 copy-done
  376.4 26.7 %all-gather.24.cloned.1.call-done = f32[3072,128]{1,0:T(8,128)} async-done(((f32[1536,128]{1,0:T(8,128)}), f32[3072,128]{1,0:T(8,128)}) %all-gather.24.cloned.1.call-update) | async-done | bytes 1572880 | tf_op jit(solution)/shard_map/all_gather | solution.py:17
  406.9 11.7 %cholesky.156 = f32[128,128]{1,0:T(8,128)S(1)} custom-call(f32[128,128]{1,0:T(8,128)S(1)} %fusion.103), custom_call_target="Cholesky" | custom-call | tf_op jit(solution)/shard_map/jit(cholesky)/cholesky | solution.py:103
  420.1 9.8 %custom-call.14 = f32[1,128,128]{1,2,0:T(8,128)S(1)} custom-call(f32[1,128,128]{2,1,0:T(8,128)S(1)} %fusion.86), custom_call_target="InvertDiagBlocksLowerTriangular" | custom-call | tf_op jit(solution)/shard_map/jit(_solve_triangular)/triangular_solve | solution.py:104
  431.0 2.6 convolution_select_fusion.5
  433.6 11.9 %convolution_subtract_fusion.5 = f32[1536,1536]{1,0:T(8,128)} fusion(f32[1536,1536]{1,0:T(8,128)} %copy-done, f32[1536,128]{1,0:T(8,128)S(1)} %convolution_select_fusion.5, f32[1536,128]{1,0:T(8,128)S(1)} %fusion.128, pred[1536]{0:T(1024)(128)(4,1)S(1)} %broadcast_bitcast_fusion.17), kind=kOutput, calls=%fused_computation.14 | convolution fusion | flops 3626434560 | bytes 20448768 | tf_op jit(solution)/shard_map/dot_general | solution.py:36
  445.5 2.6 broadcast_select_fusion.2
  448.5 26.9 %all-gather.26.cloned.1.call-done = f32[3072,128]{1,0:T(8,128)} async-done(((f32[1536,128]{1,0:T(8,128)}), f32[3072,128]{1,0:T(8,128)}) %all-gather.26.cloned.1.call-update) | async-done | bytes 1572880 | tf_op jit(solution)/shard_map/all_gather | solution.py:17
  479.2 11.7 %cholesky.167 = f32[128,128]{1,0:T(8,128)S(1)} custom-call(f32[128,128]{1,0:T(8,128)S(1)} %fusion.101), custom_call_target="Cholesky" | custom-call | tf_op jit(solution)/shard_map/jit(cholesky)/cholesky | solution.py:103
  492.4 9.8 %custom-call.15 = f32[1,128,128]{1,2,0:T(8,128)S(1)} custom-call(f32[1,128,128]{2,1,0:T(8,128)S(1)} %fusion.87), custom_call_target="InvertDiagBlocksLowerTriangular" | custom-call | tf_op jit(solution)/shard_map/jit(_solve_triangular)/triangular_solve | solution.py:104
  503.3 2.6 convolution_select_fusion.4
  505.9 10.7 %convolution_subtract_fusion.4 = f32[1536,1536]{1,0:T(8,128)S(1)} fusion(f32[1536,1536]{1,0:T(8,128)} %get-tuple-element.12, f32[1536,128]{1,0:T(8,128)S(1)} %convolution_select_fusion.4, f32[1536,128]{1,0:T(8,128)S(1)} %fusion.129, pred[1536]{0:T(1024)(128)(4,1)S(1)} %broadcast_bitcast_fusion.14), kind=kOutput, calls=%fused_computation.13 | convolution fusion | flops 3626434560 | bytes 20448768 | tf_op jit(solution)/shard_map/dot_general | solution.py:36
  517.1 3.7 copy-done.1
  522.5 26.7 %all-gather.28.cloned.1.call-done = f32[3072,128]{1,0:T(8,128)} async-done(((f32[1536,128]{1,0:T(8,128)}), f32[3072,128]{1,0:T(8,128)}) %all-gather.28.cloned.1.call-update) | async-done | bytes 1572880 | tf_op jit(solution)/shard_map/all_gather | solution.py:17
  552.9 11.7 %cholesky.178 = f32[128,128]{1,0:T(8,128)S(1)} custom-call(f32[128,128]{1,0:T(8,128)S(1)} %fusion.99), custom_call_target="Cholesky" | custom-call | tf_op jit(solution)/shard_map/jit(cholesky)/cholesky | solution.py:103
  566.1 9.8 %custom-call.16 = f32[1,128,128]{1,2,0:T(8,128)S(1)} custom-call(f32[1,128,128]{2,1,0:T(8,128)S(1)} %fusion.88), custom_call_target="InvertDiagBlocksLowerTriangular" | custom-call | tf_op jit(solution)/shard_map/jit(_solve_triangular)/triangular_solve | solution.py:104
  577.0 2.6 convolution_select_fusion.3
  579.7 11.9 %convolution_subtract_fusion.3 = f32[1536,1536]{1,0:T(8,128)} fusion(f32[1536,1536]{1,0:T(8,128)} %copy-done.1, f32[1536,128]{1,0:T(8,128)S(1)} %convolution_select_fusion.3, f32[1536,128]{1,0:T(8,128)S(1)} %fusion.130, pred[1536]{0:T(1024)(128)(4,1)S(1)} %broadcast_bitcast_fusion.11), kind=kOutput, calls=%fused_computation.12 | convolution fusion | flops 3626434560 | bytes 20448768 | tf_op jit(solution)/shard_map/dot_general | solution.py:36
  594.6 26.9 %all-gather.30.cloned.1.call-done = f32[3072,128]{1,0:T(8,128)} async-done(((f32[1536,128]{1,0:T(8,128)}), f32[3072,128]{1,0:T(8,128)}) %all-gather.30.cloned.1.call-update) | async-done | bytes 1572880 | tf_op jit(solution)/shard_map/all_gather | solution.py:17
  625.2 11.7 %cholesky.189 = f32[128,128]{1,0:T(8,128)S(1)} custom-call(f32[128,128]{1,0:T(8,128)S(1)} %fusion.97), custom_call_target="Cholesky" | custom-call | tf_op jit(solution)/shard_map/jit(cholesky)/cholesky | solution.py:103
  638.4 9.8 %custom-call.17 = f32[1,128,128]{1,2,0:T(8,128)S(1)} custom-call(f32[1,128,128]{2,1,0:T(8,128)S(1)} %fusion.89), custom_call_target="InvertDiagBlocksLowerTriangular" | custom-call | tf_op jit(solution)/shard_map/jit(_solve_triangular)/triangular_solve | solution.py:104
  649.3 2.6 convolution_select_fusion.2
  652.0 10.7 %convolution_subtract_fusion.2 = f32[1536,1536]{1,0:T(8,128)S(1)} fusion(f32[1536,1536]{1,0:T(8,128)} %get-tuple-element.10, f32[1536,128]{1,0:T(8,128)S(1)} %convolution_select_fusion.2, f32[1536,128]{1,0:T(8,128)S(1)} %fusion.131, pred[1536]{0:T(1024)(128)(4,1)S(1)} %broadcast_bitcast_fusion.8), kind=kOutput, calls=%fused_computation.11 | convolution fusion | flops 3626434560 | bytes 20448768 | tf_op jit(solution)/shard_map/dot_general | solution.py:36
  663.1 3.7 copy-done.2
  668.3 26.9 %all-gather.32.cloned.1.call-done = f32[3072,128]{1,0:T(8,128)} async-done(((f32[1536,128]{1,0:T(8,128)}), f32[3072,128]{1,0:T(8,128)}) %all-gather.32.cloned.1.call-update) | async-done | bytes 1572880 | tf_op jit(solution)/shard_map/all_gather | solution.py:17
  699.0 11.7 %cholesky.200 = f32[128,128]{1,0:T(8,128)S(1)} custom-call(f32[128,128]{1,0:T(8,128)S(1)} %fusion.95), custom_call_target="Cholesky" | custom-call | tf_op jit(solution)/shard_map/jit(cholesky)/cholesky | solution.py:103
  712.1 9.8 %custom-call.18 = f32[1,128,128]{1,2,0:T(8,128)S(1)} custom-call(f32[1,128,128]{2,1,0:T(8,128)S(1)} %fusion.90), custom_call_target="InvertDiagBlocksLowerTriangular" | custom-call | tf_op jit(solution)/shard_map/jit(_solve_triangular)/triangular_solve | solution.py:104
  723.1 2.6 convolution_select_fusion.1
  725.7 12.3 %convolution_subtract_fusion.1 = f32[1536,1536]{1,0:T(8,128)} fusion(f32[1536,1536]{1,0:T(8,128)} %copy-done.2, f32[1536,128]{1,0:T(8,128)S(1)} %convolution_select_fusion.1, f32[1536,128]{1,0:T(8,128)S(1)} %fusion.132, pred[1536]{0:T(1024)(128)(4,1)S(1)} %broadcast_bitcast_fusion.5), kind=kOutput, calls=%fused_computation.10 | convolution fusion | flops 3626434560 | bytes 20448768 | tf_op jit(solution)/shard_map/dot_general | solution.py:36
  741.0 26.9 %all-gather.34.cloned.1.call-done = f32[3072,128]{1,0:T(8,128)} async-done(((f32[1536,128]{1,0:T(8,128)}), f32[3072,128]{1,0:T(8,128)}) %all-gather.34.cloned.1.call-update) | async-done | bytes 1572880 | tf_op jit(solution)/shard_map/all_gather | solution.py:17
  771.7 11.7 %cholesky.211 = f32[128,128]{1,0:T(8,128)S(1)} custom-call(f32[128,128]{1,0:T(8,128)S(1)} %fusion.93), custom_call_target="Cholesky" | custom-call | tf_op jit(solution)/shard_map/jit(cholesky)/cholesky | solution.py:103
  784.9 9.8 %custom-call.19 = f32[1,128,128]{1,2,0:T(8,128)S(1)} custom-call(f32[1,128,128]{2,1,0:T(8,128)S(1)} %fusion.91), custom_call_target="InvertDiagBlocksLowerTriangular" | custom-call | tf_op jit(solution)/shard_map/jit(_solve_triangular)/triangular_solve | solution.py:104
  795.8 2.6 convolution_select_fusion
  798.4 10.9 %convolution_subtract_fusion = f32[1536,1536]{1,0:T(8,128)S(1)} fusion(f32[1536,1536]{1,0:T(8,128)} %get-tuple-element.8, f32[1536,128]{1,0:T(8,128)S(1)} %convolution_select_fusion, f32[1536,128]{1,0:T(8,128)S(1)} %fusion.133, pred[1536]{0:T(1024)(128)(4,1)S(1)} %broadcast_bitcast_fusion.2), kind=kOutput, calls=%fused_computation.9 | convolution fusion | flops 3626434560 | bytes 20448768 | tf_op jit(solution)/shard_map/dot_general | solution.py:36
  809.8 2.9 or_select_fusion
  812.7 11.0 %copy.44 = f32[1,12,128,1,1536]{4,3,2,1,0:T(1,128)} copy(f32[1,12,128,1,1536]{4,2,1,3,0:T(8,128)S(1)} %bitcast.211) | data formatting | bytes 18874368 | tf_op jit(solution)/shard_map/reshape | solution.py:126
  (245 shorter events, 66.8 us)
Async XLA Ops:
  6.5 27.2 %copy-start.4 = (bf16[1,1024,256]{2,1,0:T(8,128)(2,1)S(1)}, bf16[1,1024,256]{2,1,0:T(8,128)(2,1)}, u32[]{:S(2)}) copy-start(bf16[1,1024,256]{2,1,0:T(8,128)(2,1)} %param.7) | copy-start | bytes 1572868
  6.5 27.2 %all-gather.18.cloned.1.call-start = ((), (), s32[]{:S(2)}) async-start(), calls=%async_computation.1 | async-start | bytes 1572864 | tf_op jit(solution)/shard_map/all_gather | solution.py:64
  63.7 77.7 %all-to-all-start = ((bf16[1024,2,1536]{0,2,1:T(8,128)(2,1)}), bf16[1024,2,1536]{0,2,1:T(8,128)(2,1)}, u32[]{:S(2)}, u32[]{:S(2)}) async-start(bf16[1024,2,1536]{0,2,1:T(8,128)(2,1)} %select_convert_fusion), calls=%async_computation | async-start | bytes 12582912 | tf_op jit(solution)/shard_map/all_to_all | solution.py:76
  70.0 187.0 %all-gather.20.cloned.1.call-start = ((), (), s32[]{:S(2)}) async-start(), calls=%async_computation.2 | async-start | bytes 2359296 | tf_op jit(solution)/shard_map/all_gather | solution.py:17
  183.2 32.5 %collective-permute-start = (bf16[1536,1536]{1,0:T(8,128)(2,1)}, bf16[1536,1536]{1,0:T(8,128)(2,1)}, u32[]{:S(2)}, u32[]{:S(2)}) collective-permute-start(bf16[1536,1536]{1,0:T(8,128)(2,1)} %select_convert_fusion.1), channel_id=1, source_target_pairs={{0,2},{2,0},{4,6},{6,4},{8,10},{10,8},{12,14},{14,12},{16,18},{18,... | collective-permute-start | bytes 14155784 | tf_op jit(solution)/shard_map/ppermute | solution.py:12
  224.3 3.7 copy-start.3
  229.1 100.3 %all-gather.22.cloned.1.call-start = ((), (), s32[]{:S(2)}) async-start(), calls=%async_computation.3 | async-start | bytes 2359296 | tf_op jit(solution)/shard_map/all_gather | solution.py:17
  258.8 1.9 collective-permute-start.1
  260.1 24.8 %collective-permute-start.2 = (bf16[128,1536]{1,0:T(8,128)(2,1)S(1)}, bf16[128,1536]{1,0:T(8,128)(2,1)S(1)}, u32[]{:S(2)}, u32[]{:S(2)}) collective-permute-start(bf16[128,1536]{1,0:T(8,128)(2,1)S(1)} %slice.247), channel_id=1, source_target_pairs={{0,2},{2,0},{4,6},{6,4},{8,10},{10,8},{12,14},{14,12},{16,18},{18,... | collective-permute-start | bytes 1179656 | tf_op jit(solution)/shard_map/ppermute | solution.py:12
  302.1 101.1 %all-gather.24.cloned.1.call-start = ((), (), s32[]{:S(2)}) async-start(), calls=%async_computation.4 | async-start | bytes 2359296 | tf_op jit(solution)/shard_map/all_gather | solution.py:17
  331.1 1.9 collective-permute-start.3
  332.4 24.8 %collective-permute-start.4 = (bf16[128,1536]{1,0:T(8,128)(2,1)S(1)}, bf16[128,1536]{1,0:T(8,128)(2,1)S(1)}, u32[]{:S(2)}, u32[]{:S(2)}) collective-permute-start(bf16[128,1536]{1,0:T(8,128)(2,1)S(1)} %slice.246), channel_id=1, source_target_pairs={{0,2},{2,0},{4,6},{6,4},{8,10},{10,8},{12,14},{14,12},{16,18},{18,... | collective-permute-start | bytes 1179656 | tf_op jit(solution)/shard_map/ppermute | solution.py:12
  371.0 3.7 copy-start
  375.8 99.7 %all-gather.26.cloned.1.call-start = ((), (), s32[]{:S(2)}) async-start(), calls=%async_computation.5 | async-start | bytes 2359296 | tf_op jit(solution)/shard_map/all_gather | solution.py:17
  404.8 1.9 collective-permute-start.5
  406.2 24.8 %collective-permute-start.6 = (bf16[128,1536]{1,0:T(8,128)(2,1)S(1)}, bf16[128,1536]{1,0:T(8,128)(2,1)S(1)}, u32[]{:S(2)}, u32[]{:S(2)}) collective-permute-start(bf16[128,1536]{1,0:T(8,128)(2,1)S(1)} %slice.245), channel_id=1, source_target_pairs={{0,2},{2,0},{4,6},{6,4},{8,10},{10,8},{12,14},{14,12},{16,18},{18,... | collective-permute-start | bytes 1179656 | tf_op jit(solution)/shard_map/ppermute | solution.py:12
  448.1 101.1 %all-gather.28.cloned.1.call-start = ((), (), s32[]{:S(2)}) async-start(), calls=%async_computation.6 | async-start | bytes 2359296 | tf_op jit(solution)/shard_map/all_gather | solution.py:17
  477.2 1.9 collective-permute-start.7
  478.5 24.8 %collective-permute-start.8 = (bf16[128,1536]{1,0:T(8,128)(2,1)S(1)}, bf16[128,1536]{1,0:T(8,128)(2,1)S(1)}, u32[]{:S(2)}, u32[]{:S(2)}) collective-permute-start(bf16[128,1536]{1,0:T(8,128)(2,1)S(1)} %slice.244), channel_id=1, source_target_pairs={{0,2},{2,0},{4,6},{6,4},{8,10},{10,8},{12,14},{14,12},{16,18},{18,... | collective-permute-start | bytes 1179656 | tf_op jit(solution)/shard_map/ppermute | solution.py:12
  517.1 3.7 copy-start.1
  521.8 99.6 %all-gather.30.cloned.1.call-start = ((), (), s32[]{:S(2)}) async-start(), calls=%async_computation.7 | async-start | bytes 2359296 | tf_op jit(solution)/shard_map/all_gather | solution.py:17
  550.9 1.9 collective-permute-start.9
  552.2 24.8 %collective-permute-start.10 = (bf16[128,1536]{1,0:T(8,128)(2,1)S(1)}, bf16[128,1536]{1,0:T(8,128)(2,1)S(1)}, u32[]{:S(2)}, u32[]{:S(2)}) collective-permute-start(bf16[128,1536]{1,0:T(8,128)(2,1)S(1)} %slice.243), channel_id=1, source_target_pairs={{0,2},{2,0},{4,6},{6,4},{8,10},{10,8},{12,14},{14,12},{16,18},{18,... | collective-permute-start | bytes 1179656 | tf_op jit(solution)/shard_map/ppermute | solution.py:12
  594.2 101.1 %all-gather.32.cloned.1.call-start = ((), (), s32[]{:S(2)}) async-start(), calls=%async_computation.8 | async-start | bytes 2359296 | tf_op jit(solution)/shard_map/all_gather | solution.py:17
  623.2 1.9 collective-permute-start.11
  624.5 24.8 %collective-permute-start.12 = (bf16[128,1536]{1,0:T(8,128)(2,1)S(1)}, bf16[128,1536]{1,0:T(8,128)(2,1)S(1)}, u32[]{:S(2)}, u32[]{:S(2)}) collective-permute-start(bf16[128,1536]{1,0:T(8,128)(2,1)S(1)} %slice.242), channel_id=1, source_target_pairs={{0,2},{2,0},{4,6},{6,4},{8,10},{10,8},{12,14},{14,12},{16,18},{18,... | collective-permute-start | bytes 1179656 | tf_op jit(solution)/shard_map/ppermute | solution.py:12
  663.1 3.7 copy-start.2
  667.9 100.0 %all-gather.34.cloned.1.call-start = ((), (), s32[]{:S(2)}) async-start(), calls=%async_computation.9 | async-start | bytes 2359296 | tf_op jit(solution)/shard_map/all_gather | solution.py:17
  696.9 1.9 collective-permute-start.13
  698.3 24.8 %collective-permute-start.14 = (bf16[128,1536]{1,0:T(8,128)(2,1)S(1)}, bf16[128,1536]{1,0:T(8,128)(2,1)S(1)}, u32[]{:S(2)}, u32[]{:S(2)}) collective-permute-start(bf16[128,1536]{1,0:T(8,128)(2,1)S(1)} %slice.241), channel_id=1, source_target_pairs={{0,2},{2,0},{4,6},{6,4},{8,10},{10,8},{12,14},{14,12},{16,18},{18,... | collective-permute-start | bytes 1179656 | tf_op jit(solution)/shard_map/ppermute | solution.py:12
  769.7 1.9 collective-permute-start.15
  771.0 24.8 %collective-permute-start.16 = (bf16[128,1536]{1,0:T(8,128)(2,1)S(1)}, bf16[128,1536]{1,0:T(8,128)(2,1)S(1)}, u32[]{:S(2)}, u32[]{:S(2)}) collective-permute-start(bf16[128,1536]{1,0:T(8,128)(2,1)S(1)} %slice.240), channel_id=1, source_target_pairs={{0,2},{2,0},{4,6},{6,4},{8,10},{10,8},{12,14},{14,12},{16,18},{18,... | collective-permute-start | bytes 1179656 | tf_op jit(solution)/shard_map/ppermute | solution.py:12
Sparse Core Ops, SparseCore 0:
  8.9 23.9 all-gather.17
  229.2 27.8 all-gather.19
  302.2 27.1 all-gather.21
  375.9 27.1 all-gather.23
  448.2 27.1 all-gather.25
  522.0 27.1 all-gather.27
  594.3 27.1 all-gather.29
  668.0 27.1 all-gather.31
  740.7 27.1 all-gather.33
